TPU v7x, 512 devices: a whole 4x8x8 slice. The times are simulated.
512 devices in a mesh: mem: 4 (over x), lat: 4 (over y_hi, core), lon: 32 (over z, y_lo).
Axes of the slice: x: 4, y: 8 (y_hi: 2, y_lo: 4; y = y_hi * 4 + y_lo), z: 8, core: 2. Of those that a mesh axis runs over, the one named last changes fastest.
Arguments:
- initial_temp: float32 [100, 128, 512], P(None, 'lon', 'lat'), may hold values from -6 to 6
- land_mask: int32 [128, 512], P('lon', 'lat'), may hold values 0 or 1
- pert_table: float32 [16, 100], replicated, may hold values from 0.03 to 0.24
- pert_index: int32 [8], P('mem'), may hold values from 0 to 15
- base_kh: float32 [100], replicated, may hold values from 0.03 to 0.24
- member_mix: bfloat16 [8, 100, 100], P('mem'), may hold values from -0.15625 to 0.15625
- base_mix: bfloat16 [100, 100], replicated, may hold values from -0.15625 to 0.15625
- owner: int32 [32768, 1], P(('lat', 'lon')), may hold values from 0 to 127; in each aligned block of 256 rows (0 to 255, 256 to 511, ...) at most 4 rows name the same one
- column: int32 [32768], P(('lat', 'lon')), may hold values from 0 to 511
- interp_w: float32 [32768, 100], P(('lat', 'lon')), may hold values from 0 to 1
- obs_inv_var: float32 [32768, 100], P(('lat', 'lon')), may hold values from 1 to 16
- observed: float32 [32768, 100], P(('lat', 'lon')), may hold values from -6 to 6
Outputs:
- member_temp: bfloat16 [8, 100, 128, 512], P('mem', None, 'lon', 'lat')
- base_temp: bfloat16 [100, 128, 512], P(None, 'lon', 'lat')
- gram_block: float32 [8, 8], replicated
- projection: float32 [8], replicated
- misfit: float32 [32768, 100], P(('lat', 'lon'))
Inputs may be any that keep to these rules, and one draw needn't show every extreme that they name: Within the records of one device no owner is named more than 4 times, and in every draw some owner is named exactly 4 times by some device's records. The column within the owner's block is the longitude offset times 128 plus the latitude offset.
All inputs are finite; a program needn't handle non-finite values. No bound on the sum of `land_mask` on one device may be relied on, other than what follows from the above.
Results may differ from a plain program's by a relative error of at most 0.012.
Values may be sent and summed in bfloat16 or wider, within the bound.
No kernel may reach another device: no remote copies, remote signals or barrier semaphores. Data moves between devices by JAX's collectives and lax.ppermute only.
A program may use at most 64 MiB of HBM per device.

v0:
```python
import jax
import jax.numpy as jnp
from jax import lax
from jax.sharding import PartitionSpec as P

STEPS = 5


def padded_2(cells, sides, width, closed):
    for axis, dim in sides:
        count = lax.axis_size(axis)
        ends = count if closed else count - 1
        head = lax.slice_in_dim(cells, 0, width, axis=dim)
        tail = lax.slice_in_dim(cells, cells.shape[dim] - width, cells.shape[dim], axis=dim)
        cells = jnp.concatenate(
            [
                lax.ppermute(tail, axis, [(i, (i + 1) % count) for i in range(ends)]),
                cells,
                lax.ppermute(head, axis, [((i + 1) % count, i) for i in range(ends)]),
            ],
            axis=dim,
        )
    return cells


def on_device(
    initial_temp,
    land_mask,
    pert_table,
    pert_index,
    base_kh,
    member_mix,
    base_mix,
    owner,
    column,
    interp_w,
    obs_inv_var,
    observed,
):
    members = pert_index.shape[0]
    levels = initial_temp.shape[0]
    width_lon = initial_temp.shape[1]
    width_lat = initial_temp.shape[2]
    table_rows = pert_table.shape[0]
    chooser = (pert_index[:, None] == jnp.arange(table_rows)[None, :]).astype(jnp.float32)
    member_kh = jnp.dot(chooser, pert_table, precision=lax.Precision.HIGHEST)
    run_kh = jnp.concatenate([member_kh, base_kh[None, :]], 0)
    run_mix = jnp.concatenate([member_mix, base_mix[None]], 0)
    run_count = members + 1
    fields = jnp.broadcast_to(
        initial_temp.astype(jnp.bfloat16)[None], (run_count, levels, width_lon, width_lat)
    )
    total_lat = width_lat * lax.axis_size("lat")
    lat_start = lax.axis_index("lat") * width_lat
    ocean_open = land_mask.astype(jnp.float32)
    for step_index in range(STEPS):
        lon_padded = padded_2(fields, (("lon", 2),), 1, True)
        padded = padded_2(lon_padded, (("lat", 3),), 1, False)
        global_rows = lat_start - (1 - 1) + jnp.arange(width_lat + 2 * (1 - 1))
        has_next = (global_rows < total_lat - 1).astype(jnp.float32)
        has_prior = (global_rows > 0).astype(jnp.float32)
        widened = padded.astype(jnp.float32)
        values = widened[:, :, 1:-1, 1:-1]
        laplace = widened[:, :, 2:, 1:-1] + widened[:, :, :-2, 1:-1] - 2.0 * values
        laplace = (
            laplace
            + has_next * (widened[:, :, 1:-1, 2:] - values)
            + has_prior * (widened[:, :, 1:-1, :-2] - values)
        )
        right_side = (values + run_kh[:, :, None, None] * laplace).astype(jnp.bfloat16)
        vertical = right_side.astype(jnp.float32) + jnp.einsum(
            "rkj,rjab->rkab", run_mix, right_side, preferred_element_type=jnp.float32
        )
        fields = (values + ocean_open * (vertical - values)).astype(jnp.bfloat16)
    owners = lax.axis_size("lat") * lax.axis_size("lon")
    prof_dev = owner.shape[0]
    capacity = max(2, 2 * prof_dev // owners)
    target = owner[:, 0]
    matches = (target[:, None] == jnp.arange(owners)[None, :]).astype(jnp.int32)
    earlier = jnp.cumsum(matches, 0) - matches
    slot_rank = jnp.sum(earlier * matches, 1)
    position = target * capacity + slot_rank
    send_ids = (
        jnp.full((owners * capacity,), -1, jnp.int32)
        .at[position]
        .set(column)
        .reshape(owners, capacity)
    )
    records = jnp.stack([interp_w, obs_inv_var, observed], 1)
    send_records = (
        jnp.zeros((owners * capacity, 3, levels), jnp.float32)
        .at[position]
        .set(records)
        .reshape(owners, capacity, 3, levels)
    )
    columns_flat = fields.reshape(run_count, levels, width_lon * width_lat)
    column_ids = lax.all_to_all(send_ids, ("lat", "lon"), split_axis=0, concat_axis=0, tiled=True)
    record_rows = lax.all_to_all(
        send_records, ("lat", "lon"), split_axis=0, concat_axis=0, tiled=True
    )
    sources = column_ids.shape[0]
    slot_count = column_ids.shape[1]
    usable = (column_ids >= 0).astype(jnp.float32).reshape(-1)
    picked = jnp.take(columns_flat, jnp.maximum(column_ids, 0).reshape(-1), axis=2).astype(
        jnp.float32
    )
    deeper = jnp.concatenate([picked[:, 1:], picked[:, -1:]], 1)
    flat_records = record_rows.reshape(sources * slot_count, 3, levels)
    weight = flat_records[:, 0].T
    inv_var = flat_records[:, 1].T * usable
    measured = flat_records[:, 2].T
    modeled = weight * picked + (1.0 - weight) * deeper
    green_cols = ((modeled[:members] - modeled[members]) * usable).astype(jnp.bfloat16)
    misfit = (measured - modeled[members]) * usable
    extras = jnp.stack([inv_var, misfit], 0)
    green_cols, extras = (
        green_cols.reshape(members, levels, sources, slot_count),
        extras.reshape(2, levels, sources, slot_count),
    )
    owner_misfit = jnp.transpose(extras[1], (1, 2, 0))
    returned = lax.all_to_all(owner_misfit, ("lat", "lon"), split_axis=0, concat_axis=0, tiled=True)
    misfit_rows = jnp.take(returned.reshape(owners * capacity, levels), position, axis=0)
    green_cols = green_cols.reshape(members, levels, -1)
    extras = extras.reshape(2, levels, -1)
    normalizer = 1.0 / (prof_dev * owners * levels)
    green_all = lax.all_gather(green_cols, "mem", axis=0, tiled=True)
    green_float = green_all.astype(jnp.float32)
    weighted = green_float * extras[0]
    gram_part = (
        jnp.einsum("mks,nks->mn", weighted, green_float, precision=lax.Precision.HIGHEST)
        * normalizer
    )
    proj_part = (
        jnp.einsum("mks,ks->m", weighted, extras[1], precision=lax.Precision.HIGHEST) * normalizer
    )
    gram_part, proj_part = (gram_part, proj_part)
    gram_block, projection = lax.psum((gram_part, proj_part), ("lat", "lon"))
    return (fields[:members], fields[members], gram_block, projection, misfit_rows)


def solution(mesh):
    placed = (
        P(None, "lon", "lat"),
        P("lon", "lat"),
        P(),
        P("mem"),
        P(),
        P("mem", None, None),
        P(),
        P(("lat", "lon"), None),
        P(("lat", "lon")),
        P(("lat", "lon"), None),
        P(("lat", "lon"), None),
        P(("lat", "lon"), None),
    )
    return jax.shard_map(
        on_device,
        mesh=mesh,
        in_specs=placed,
        out_specs=(
            P("mem", None, "lon", "lat"),
            P(None, "lon", "lat"),
            P(),
            P(),
            P(("lat", "lon"), None),
        ),
        check_vma=False,
    )
```

profile of v0, /device:TPU:258, one launch (start us, length us, event | category | flops | bytes accessed | tf_op | source)
XLA Modules:
  0.0 559.3 jit_solution(4841442048766482967)
XLA Ops:
  1.6 4.6 collective-permute-start.1
  6.3 1.9 collective-permute-start
  10.8 5.7 %collective-permute-done = bf16[3,100,1,128]{3,1,2,0:T(8,128)(2,1)S(1)} collective-permute-done((bf16[3,100,1,128]{3,1,2,0:T(8,128)(2,1)S(1)}, bf16[3,100,1,128]{3,1,2,0:T(8,128)(2,1)S(1)}, u32[]{:S(2)}, u32[]{:S(2)}) %collective-permute-start) | collective-permute-done | bytes 76832 | tf_op jit(solution)/shard_map/ppermute | solution.py:17
  19.6 5.7 %collective-permute-done.3 = bf16[3,100,6,1]{3,1,2,0:T(8,128)(2,1)S(1)} collective-permute-done((bf16[3,100,6,1]{3,1,2,0:T(8,128)(2,1)S(1)}, bf16[3,100,6,1]{3,1,2,0:T(8,128)(2,1)S(1)}, u32[]{:S(2)}, u32[]{:S(2)}) %collective-permute-start.3) | collective-permute-done | bytes 3632 | tf_op jit(solution)/shard_map/ppermute | solution.py:19
  27.4 1.9 collective-permute-start.4
  29.4 7.8 %collective-permute-start.5 = (bf16[3,100,1,128]{3,1,2,0:T(8,128)(2,1)S(1)}, bf16[3,100,1,128]{3,1,2,0:T(8,128)(2,1)S(1)}, u32[]{:S(2)}, u32[]{:S(2)}) collective-permute-start(bf16[3,100,1,128]{3,1,2,0:T(8,128)(2,1)S(1)} %get-tuple-element.41), channel_id=1, source_target_pairs={{1,0},{2,1},{3,2},{4,3},{5,4},{6,5},{7,6},{8,7},{9,8},{10,9},{11,1... | collective-permute-start | bytes 230408 | tf_op jit(solution)/shard_map/ppermute | solution.py:19
  39.5 13.3 %collective-permute-start.6 = (bf16[3,100,6,1]{3,1,2,0:T(8,128)(2,1)S(1)}, bf16[3,100,6,1]{3,1,2,0:T(8,128)(2,1)S(1)}, u32[]{:S(2)}, u32[]{:S(2)}) collective-permute-start(bf16[3,100,6,1]{3,1,2,0:T(8,128)(2,1)S(1)} %get-tuple-element.30), channel_id=1, source_target_pairs={{0,32},{32,64},{64,96},{1,33},{33,65},{65,97},{2,34},{34,66},{66,9... | collective-permute-start | bytes 10808 | tf_op jit(solution)/shard_map/ppermute | solution.py:17
  56.4 18.1 %all-to-all-start.1 = ((s32[128,1,4]{2,1,0:T(1,128)}), s32[128,1,4]{2,1,0:T(1,128)S(1)}, u32[]{:S(2)}, u32[]{:S(2)}) async-start(s32[128,1,4]{2,1,0:T(1,128)} %bitcast.22), calls=%async_computation.1 | async-start | bytes 131072 | tf_op jit(solution)/shard_map/all_to_all | solution.py:97
  75.2 1.6 fusion.20
  76.8 3.4 collective-permute-start.8
  80.2 6.4 %collective-permute-start.9 = (bf16[3,100,1,128]{3,1,2,0:T(8,128)(2,1)S(1)}, bf16[3,100,1,128]{3,1,2,0:T(8,128)(2,1)S(1)}, u32[]{:S(2)}, u32[]{:S(2)}) collective-permute-start(bf16[3,100,1,128]{3,1,2,0:T(8,128)(2,1)S(1)} %get-tuple-element.39), channel_id=1, source_target_pairs={{1,0},{2,1},{3,2},{4,3},{5,4},{6,5},{7,6},{8,7},{9,8},{10,9},{11,1... | collective-permute-start | bytes 230408 | tf_op jit(solution)/shard_map/ppermute | solution.py:19
  93.0 7.1 %scatter_fusion = f32[512,3,100]{2,1,0:T(4,128)S(1)} fusion(f32[512,3,100]{2,1,0:T(4,128)S(1)} %broadcast_in_dim.33, s32[256]{0:T(256)S(1)} %bitcast.104, f32[256,3,100]{2,1,0:T(4,128)S(1)} %copy.45), kind=kCustom, calls=%fused_computation.2 | custom fusion | bytes 922624 | tf_op jit(solution)/shard_map/scatter | solution.py:93
  103.3 1.9 collective-permute-start.12
  105.2 8.2 %collective-permute-start.13 = (bf16[3,100,1,128]{3,1,2,0:T(8,128)(2,1)S(1)}, bf16[3,100,1,128]{3,1,2,0:T(8,128)(2,1)S(1)}, u32[]{:S(2)}, u32[]{:S(2)}) collective-permute-start(bf16[3,100,1,128]{3,1,2,0:T(8,128)(2,1)S(1)} %get-tuple-element.37), channel_id=1, source_target_pairs={{1,0},{2,1},{3,2},{4,3},{5,4},{6,5},{7,6},{8,7},{9,8},{10,9},{11,1... | collective-permute-start | bytes 230408 | tf_op jit(solution)/shard_map/ppermute | solution.py:19
  113.4 21.5 %all-to-all-start = ((f32[128,4,3,100]{3,1,2,0:T(4,128)}), f32[128,4,3,100]{3,1,2,0:T(4,128)S(1)}, u32[]{:S(2)}, u32[]{:S(2)}) async-start(f32[128,4,3,100]{3,1,2,0:T(4,128)} %copy.47), calls=%async_computation | async-start | bytes 1572864 | tf_op jit(solution)/shard_map/all_to_all | solution.py:98
  135.5 2.3 collective-permute-start.14
  140.1 6.5 %collective-permute-done.15 = bf16[3,100,6,1]{3,1,2,0:T(8,128)(2,1)} collective-permute-done((bf16[3,100,6,1]{3,1,2,0:T(8,128)(2,1)S(1)}, bf16[3,100,6,1]{3,1,2,0:T(8,128)(2,1)}, u32[]{:S(2)}, u32[]{:S(2)}) %collective-permute-start.15) | collective-permute-done | bytes 3632 | tf_op jit(solution)/shard_map/ppermute | solution.py:19
  146.7 1.7 maximum_convert_fusion.3
  150.0 2.5 collective-permute-start.16
  152.5 7.3 %collective-permute-start.17 = (bf16[3,100,1,128]{3,1,2,0:T(8,128)(2,1)S(1)}, bf16[3,100,1,128]{3,1,2,0:T(8,128)(2,1)S(1)}, u32[]{:S(2)}, u32[]{:S(2)}) collective-permute-start(bf16[3,100,1,128]{3,1,2,0:T(8,128)(2,1)S(1)} %get-tuple-element.35), channel_id=1, source_target_pairs={{1,0},{2,1},{3,2},{4,3},{5,4},{6,5},{7,6},{8,7},{9,8},{10,9},{11,1... | collective-permute-start | bytes 230408 | tf_op jit(solution)/shard_map/ppermute | solution.py:19
  160.0 1.6 collective-permute-done.16
  162.1 23.8 %collective-permute-start.18 = (bf16[3,100,6,1]{3,1,2,0:T(8,128)(2,1)S(1)}, bf16[3,100,6,1]{3,1,2,0:T(8,128)(2,1)S(1)}, u32[]{:S(2)}, u32[]{:S(2)}) collective-permute-start(bf16[3,100,6,1]{3,1,2,0:T(8,128)(2,1)S(1)} %get-tuple-element.24), channel_id=1, source_target_pairs={{0,32},{32,64},{64,96},{1,33},{33,65},{65,97},{2,34},{34,66},{66,9... | collective-permute-start | bytes 10808 | tf_op jit(solution)/shard_map/ppermute | solution.py:17
  188.5 1.7 collective-permute-done.19
  190.2 1.7 maximum_convert_fusion.4
  194.3 2.1 gather_fusion
  196.4 1.8 convert_bitcast_fusion
  201.2 1.9 fusion.36
  206.1 24.3 %all-to-all-start.2 = ((f32[128,4,100]{2,1,0:T(4,128)}), f32[128,4,100]{2,1,0:T(4,128)S(1)}, u32[]{:S(2)}, u32[]{:S(2)}) async-start(f32[128,4,100]{2,1,0:T(4,128)} %bitcast.35), calls=%async_computation.2 | async-start | bytes 524288 | tf_op jit(solution)/shard_map/all_to_all | solution.py:121
  231.5 14.8 %all_gather.3 = bf16[8,100,512]{2,1,0:T(8,128)(2,1)S(1)} all-gather(bf16[2,100,512]{2,1,0:T(8,128)(2,1)S(1)} %copy.52), channel_id=1, replica_groups=mesh['mem'=4,'lat'=4,'lon'=32] {'mem'}, dimensions={0}, use_global_device_ids=true | all-gather | bytes 1024000 | tf_op jit(solution)/shard_map/all_gather | solution.py:126
  246.6 3.9 fusion.33
  250.4 2.6 fusion.27
  253.0 304.7 %all-reduce = (f32[8,8]{1,0:T(8,128)}, f32[8]{0:T(128)}) all-reduce(f32[8,8]{1,0:T(8,128)S(1)} %fusion.27, f32[8]{0:T(128)S(1)} %fusion.33), channel_id=1, replica_groups=mesh['mem'=4,'lat'=4,'lon'=32] {'lat','lon'}, use_global_device_ids=true, to_apply=%region_5.6 | all-reduce | flops 72 | bytes 576 | tf_op jit(solution)/shard_map/psum | solution.py:137
  (126 shorter events, 43.7 us)
Async XLA Ops:
  0.6 8.6 %copy-start = (f32[16,100]{1,0:T(8,128)S(1)}, f32[16,100]{1,0:T(8,128)}, u32[]{:S(2)}) copy-start(f32[16,100]{1,0:T(8,128)} %param.14) | copy-start | bytes 19204
  1.6 9.2 %collective-permute-start.1 = (bf16[3,100,1,128]{3,1,2,0:T(8,128)(2,1)S(1)}, bf16[3,100,1,128]{3,1,2,0:T(8,128)(2,1)S(1)}, u32[]{:S(2)}, u32[]{:S(2)}) collective-permute-start(bf16[3,100,1,128]{3,1,2,0:T(8,128)(2,1)S(1)} %broadcast_in_dim.30), channel_id=1, source_target_pairs={{1,0},{2,1},{3,2},{4,3},{5,4},{6,5},{7,6},{8,7},{9,8},{10,9},{11,1... | collective-permute-start | bytes 230408 | tf_op jit(solution)/shard_map/ppermute | solution.py:19
  6.3 10.2 %collective-permute-start = (bf16[3,100,1,128]{3,1,2,0:T(8,128)(2,1)S(1)}, bf16[3,100,1,128]{3,1,2,0:T(8,128)(2,1)S(1)}, u32[]{:S(2)}, u32[]{:S(2)}) collective-permute-start(bf16[3,100,1,128]{3,1,2,0:T(8,128)(2,1)S(1)} %broadcast_in_dim.28), channel_id=1, source_target_pairs={{0,1},{1,2},{2,3},{3,4},{4,5},{5,6},{6,7},{7,8},{8,9},{9,10},{10,1... | collective-permute-start | bytes 230408 | tf_op jit(solution)/shard_map/ppermute | solution.py:17
  9.0 10.5 %copy-start.10 = (s32[4,128]{1,0:T(4,128)S(1)}, s32[4,128]{1,0:T(4,128)}, u32[]{:S(2)}) copy-start(s32[4,128]{1,0:T(4,128)} %param.13) | copy-start | bytes 6148
  9.0 10.5 %copy-start.8 = (bf16[2,100,100]{2,0,1:T(2,128)(2,1)S(1)}, bf16[2,100,100]{2,0,1:T(2,128)(2,1)}, u32[]{:S(2)}) copy-start(bf16[2,100,100]{2,0,1:T(2,128)(2,1)} %param.17) | copy-start | bytes 120004
  16.8 9.0 %copy-start.11 = (bf16[100,100]{1,0:T(8,128)(2,1)S(1)}, bf16[100,100]{1,0:T(8,128)(2,1)}, u32[]{:S(2)}) copy-start(bf16[100,100]{1,0:T(8,128)(2,1)} %param.18) | copy-start | bytes 60004
  16.8 2.8 collective-permute-start.2
  18.1 7.1 %collective-permute-start.3 = (bf16[3,100,6,1]{3,1,2,0:T(8,128)(2,1)S(1)}, bf16[3,100,6,1]{3,1,2,0:T(8,128)(2,1)S(1)}, u32[]{:S(2)}, u32[]{:S(2)}) collective-permute-start(bf16[3,100,6,1]{3,1,2,0:T(8,128)(2,1)S(1)} %get-tuple-element.33), channel_id=1, source_target_pairs={{32,0},{64,32},{96,64},{33,1},{65,33},{97,65},{34,2},{66,34},{98,6... | collective-permute-start | bytes 10808 | tf_op jit(solution)/shard_map/ppermute | solution.py:19
  25.8 11.4 %copy-start.9 = (s32[256,1]{0,1:T(1,128)S(1)}, s32[256,1]{0,1:T(1,128)}, u32[]{:S(2)}) copy-start(s32[256,1]{0,1:T(1,128)} %param.19) | copy-start | bytes 3076
  27.4 10.2 %collective-permute-start.4 = (bf16[3,100,1,128]{3,1,2,0:T(8,128)(2,1)S(1)}, bf16[3,100,1,128]{3,1,2,0:T(8,128)(2,1)S(1)}, u32[]{:S(2)}, u32[]{:S(2)}) collective-permute-start(bf16[3,100,1,128]{3,1,2,0:T(8,128)(2,1)S(1)} %get-tuple-element.40), channel_id=1, source_target_pairs={{0,1},{1,2},{2,3},{3,4},{4,5},{5,6},{6,7},{7,8},{8,9},{9,10},{10,1... | collective-permute-start | bytes 230408 | tf_op jit(solution)/shard_map/ppermute | solution.py:17
  29.4 9.9 %collective-permute-start.5 = (bf16[3,100,1,128]{3,1,2,0:T(8,128)(2,1)S(1)}, bf16[3,100,1,128]{3,1,2,0:T(8,128)(2,1)S(1)}, u32[]{:S(2)}, u32[]{:S(2)}) collective-permute-start(bf16[3,100,1,128]{3,1,2,0:T(8,128)(2,1)S(1)} %get-tuple-element.41), channel_id=1, source_target_pairs={{1,0},{2,1},{3,2},{4,3},{5,4},{6,5},{7,6},{8,7},{9,8},{10,9},{11,1... | collective-permute-start | bytes 230408 | tf_op jit(solution)/shard_map/ppermute | solution.py:19
  39.5 35.1 %collective-permute-start.6 = (bf16[3,100,6,1]{3,1,2,0:T(8,128)(2,1)S(1)}, bf16[3,100,6,1]{3,1,2,0:T(8,128)(2,1)S(1)}, u32[]{:S(2)}, u32[]{:S(2)}) collective-permute-start(bf16[3,100,6,1]{3,1,2,0:T(8,128)(2,1)S(1)} %get-tuple-element.30), channel_id=1, source_target_pairs={{0,32},{32,64},{64,96},{1,33},{33,65},{65,97},{2,34},{34,66},{66,9... | collective-permute-start | bytes 10808 | tf_op jit(solution)/shard_map/ppermute | solution.py:17
  52.8 21.8 %collective-permute-start.7 = (bf16[3,100,6,1]{3,1,2,0:T(8,128)(2,1)S(1)}, bf16[3,100,6,1]{3,1,2,0:T(8,128)(2,1)S(1)}, u32[]{:S(2)}, u32[]{:S(2)}) collective-permute-start(bf16[3,100,6,1]{3,1,2,0:T(8,128)(2,1)S(1)} %get-tuple-element.31), channel_id=1, source_target_pairs={{32,0},{64,32},{96,64},{33,1},{65,33},{97,65},{34,2},{66,34},{98,6... | collective-permute-start | bytes 10808 | tf_op jit(solution)/shard_map/ppermute | solution.py:19
  56.4 57.0 %all-to-all-start.1 = ((s32[128,1,4]{2,1,0:T(1,128)}), s32[128,1,4]{2,1,0:T(1,128)S(1)}, u32[]{:S(2)}, u32[]{:S(2)}) async-start(s32[128,1,4]{2,1,0:T(1,128)} %bitcast.22), calls=%async_computation.1 | async-start | bytes 131072 | tf_op jit(solution)/shard_map/all_to_all | solution.py:97
  75.1 11.4 %copy-start.5 = (f32[256,100]{0,1:T(8,128)S(1)}, f32[256,100]{0,1:T(8,128)}, u32[]{:S(2)}) copy-start(f32[256,100]{0,1:T(8,128)} %param.23) | copy-start | bytes 307204
  75.1 11.4 %copy-start.6 = (f32[256,100]{0,1:T(8,128)S(1)}, f32[256,100]{0,1:T(8,128)}, u32[]{:S(2)}) copy-start(f32[256,100]{0,1:T(8,128)} %param.22) | copy-start | bytes 307204
  75.1 11.4 %copy-start.7 = (f32[256,100]{0,1:T(8,128)S(1)}, f32[256,100]{0,1:T(8,128)}, u32[]{:S(2)}) copy-start(f32[256,100]{0,1:T(8,128)} %param.21) | copy-start | bytes 307204
  76.8 10.5 %collective-permute-start.8 = (bf16[3,100,1,128]{3,1,2,0:T(8,128)(2,1)S(1)}, bf16[3,100,1,128]{3,1,2,0:T(8,128)(2,1)S(1)}, u32[]{:S(2)}, u32[]{:S(2)}) collective-permute-start(bf16[3,100,1,128]{3,1,2,0:T(8,128)(2,1)S(1)} %get-tuple-element.38), channel_id=1, source_target_pairs={{0,1},{1,2},{2,3},{3,4},{4,5},{5,6},{6,7},{7,8},{8,9},{9,10},{10,1... | collective-permute-start | bytes 230408 | tf_op jit(solution)/shard_map/ppermute | solution.py:17
  80.2 8.4 %collective-permute-start.9 = (bf16[3,100,1,128]{3,1,2,0:T(8,128)(2,1)S(1)}, bf16[3,100,1,128]{3,1,2,0:T(8,128)(2,1)S(1)}, u32[]{:S(2)}, u32[]{:S(2)}) collective-permute-start(bf16[3,100,1,128]{3,1,2,0:T(8,128)(2,1)S(1)} %get-tuple-element.39), channel_id=1, source_target_pairs={{1,0},{2,1},{3,2},{4,3},{5,4},{6,5},{7,6},{8,7},{9,8},{10,9},{11,1... | collective-permute-start | bytes 230408 | tf_op jit(solution)/shard_map/ppermute | solution.py:19
  89.8 11.4 %collective-permute-start.10 = (bf16[3,100,6,1]{3,1,2,0:T(8,128)(2,1)}, bf16[3,100,6,1]{3,1,2,0:T(8,128)(2,1)S(1)}, u32[]{:S(2)}, u32[]{:S(2)}) collective-permute-start(bf16[3,100,6,1]{3,1,2,0:T(8,128)(2,1)} %get-tuple-element.28), channel_id=1, source_target_pairs={{0,32},{32,64},{64,96},{1,33},{33,65},{65,97},{2,34},{34,66},{66,9... | collective-permute-start | bytes 10808 | tf_op jit(solution)/shard_map/ppermute | solution.py:17
  91.1 10.1 %collective-permute-start.11 = (bf16[3,100,6,1]{3,1,2,0:T(8,128)(2,1)}, bf16[3,100,6,1]{3,1,2,0:T(8,128)(2,1)S(1)}, u32[]{:S(2)}, u32[]{:S(2)}) collective-permute-start(bf16[3,100,6,1]{3,1,2,0:T(8,128)(2,1)} %get-tuple-element.29), channel_id=1, source_target_pairs={{32,0},{64,32},{96,64},{33,1},{65,33},{97,65},{34,2},{66,34},{98,6... | collective-permute-start | bytes 10808 | tf_op jit(solution)/shard_map/ppermute | solution.py:19
  103.3 31.9 %collective-permute-start.12 = (bf16[3,100,1,128]{3,1,2,0:T(8,128)(2,1)S(1)}, bf16[3,100,1,128]{3,1,2,0:T(8,128)(2,1)S(1)}, u32[]{:S(2)}, u32[]{:S(2)}) collective-permute-start(bf16[3,100,1,128]{3,1,2,0:T(8,128)(2,1)S(1)} %get-tuple-element.36), channel_id=1, source_target_pairs={{0,1},{1,2},{2,3},{3,4},{4,5},{5,6},{6,7},{7,8},{8,9},{9,10},{10,1... | collective-permute-start | bytes 230408 | tf_op jit(solution)/shard_map/ppermute | solution.py:17
  105.2 30.0 %collective-permute-start.13 = (bf16[3,100,1,128]{3,1,2,0:T(8,128)(2,1)S(1)}, bf16[3,100,1,128]{3,1,2,0:T(8,128)(2,1)S(1)}, u32[]{:S(2)}, u32[]{:S(2)}) collective-permute-start(bf16[3,100,1,128]{3,1,2,0:T(8,128)(2,1)S(1)} %get-tuple-element.37), channel_id=1, source_target_pairs={{1,0},{2,1},{3,2},{4,3},{5,4},{6,5},{7,6},{8,7},{9,8},{10,9},{11,1... | collective-permute-start | bytes 230408 | tf_op jit(solution)/shard_map/ppermute | solution.py:19
  113.4 87.4 %all-to-all-start = ((f32[128,4,3,100]{3,1,2,0:T(4,128)}), f32[128,4,3,100]{3,1,2,0:T(4,128)S(1)}, u32[]{:S(2)}, u32[]{:S(2)}) async-start(f32[128,4,3,100]{3,1,2,0:T(4,128)} %copy.47), calls=%async_computation | async-start | bytes 1572864 | tf_op jit(solution)/shard_map/all_to_all | solution.py:98
  135.5 3.9 collective-permute-start.14
  137.8 8.9 %collective-permute-start.15 = (bf16[3,100,6,1]{3,1,2,0:T(8,128)(2,1)S(1)}, bf16[3,100,6,1]{3,1,2,0:T(8,128)(2,1)}, u32[]{:S(2)}, u32[]{:S(2)}) collective-permute-start(bf16[3,100,6,1]{3,1,2,0:T(8,128)(2,1)S(1)} %get-tuple-element.27), channel_id=1, source_target_pairs={{32,0},{64,32},{96,64},{33,1},{65,33},{97,65},{34,2},{66,34},{98,6... | collective-permute-start | bytes 10808 | tf_op jit(solution)/shard_map/ppermute | solution.py:19
  150.0 11.6 %collective-permute-start.16 = (bf16[3,100,1,128]{3,1,2,0:T(8,128)(2,1)S(1)}, bf16[3,100,1,128]{3,1,2,0:T(8,128)(2,1)S(1)}, u32[]{:S(2)}, u32[]{:S(2)}) collective-permute-start(bf16[3,100,1,128]{3,1,2,0:T(8,128)(2,1)S(1)} %get-tuple-element.34), channel_id=1, source_target_pairs={{0,1},{1,2},{2,3},{3,4},{4,5},{5,6},{6,7},{7,8},{8,9},{9,10},{10,1... | collective-permute-start | bytes 230408 | tf_op jit(solution)/shard_map/ppermute | solution.py:17
  152.5 9.4 %collective-permute-start.17 = (bf16[3,100,1,128]{3,1,2,0:T(8,128)(2,1)S(1)}, bf16[3,100,1,128]{3,1,2,0:T(8,128)(2,1)S(1)}, u32[]{:S(2)}, u32[]{:S(2)}) collective-permute-start(bf16[3,100,1,128]{3,1,2,0:T(8,128)(2,1)S(1)} %get-tuple-element.35), channel_id=1, source_target_pairs={{1,0},{2,1},{3,2},{4,3},{5,4},{6,5},{7,6},{8,7},{9,8},{10,9},{11,1... | collective-permute-start | bytes 230408 | tf_op jit(solution)/shard_map/ppermute | solution.py:19
  162.1 25.6 %collective-permute-start.18 = (bf16[3,100,6,1]{3,1,2,0:T(8,128)(2,1)S(1)}, bf16[3,100,6,1]{3,1,2,0:T(8,128)(2,1)S(1)}, u32[]{:S(2)}, u32[]{:S(2)}) collective-permute-start(bf16[3,100,6,1]{3,1,2,0:T(8,128)(2,1)S(1)} %get-tuple-element.24), channel_id=1, source_target_pairs={{0,32},{32,64},{64,96},{1,33},{33,65},{65,97},{2,34},{34,66},{66,9... | collective-permute-start | bytes 10808 | tf_op jit(solution)/shard_map/ppermute | solution.py:17
  186.0 4.2 collective-permute-start.19
  198.1 1.9 slice-start
  206.1 351.7 %all-to-all-start.2 = ((f32[128,4,100]{2,1,0:T(4,128)}), f32[128,4,100]{2,1,0:T(4,128)S(1)}, u32[]{:S(2)}, u32[]{:S(2)}) async-start(f32[128,4,100]{2,1,0:T(4,128)} %bitcast.35), calls=%async_computation.2 | async-start | bytes 524288 | tf_op jit(solution)/shard_map/all_to_all | solution.py:121
  (4 other events, 3.5 us)
where the time goes:
time: 560 us; the launch traced here: 559 us
  blocking collectives  320 us (57%)
  starting transfers between devices  159 us (28%)
  local copies, waits for them, and re-layouts  25.4 us (5%)
  waiting for transfers between devices  25.4 us (5%)
  matrix products  15.2 us (3%)
  other arithmetic  13.8 us (2%)
    psum x1, blocking collectives, on_device(): gram_block, projection = lax.psum((gram_part, proj_part), ('lat', 'lon'))  305 us
    ppermute x10, starting transfers between devices, padded_2(): lax.ppermute(tail, axis, [(i, (i + 1) % count) for i in range(ends)])  53.6 us
    ppermute x10, starting transfers between devices, padded_2(): lax.ppermute(head, axis, [((i + 1) % count, i) for i in range(ends)])  41.1 us
    all_to_all x1, starting transfers between devices, on_device(): lax.all_to_all(owner_misfit, ('lat', 'lon'), split_axis=0, concat_axis=0,...  24.3 us
    all_to_all x1, starting transfers between devices, on_device(): lax.all_to_all(send_records, ('lat', 'lon'), split_axis=0, concat_axis=0,...  21.5 us
    all_to_all x1, starting transfers between devices, on_device(): lax.all_to_all(send_ids, ('lat', 'lon'), split_axis=0, concat_axis=0, til...  18.1 us
    ppermute x10, waiting for transfers between devices, padded_2(): lax.ppermute(head, axis, [((i + 1) % count, i) for i in range(ends)])  17.1 us
    all_gather x1, blocking collectives, on_device(): green_all = lax.all_gather(green_cols, 'mem', axis=0, tiled=True)  14.8 us
  transfers between devices with their start and end apart: 23, of which 10 were waited for; matrix products, arithmetic and copies ran while one was open for 7% of the time, Pallas kernels for 0%

commit v1 on v0

--- a/solution.py
+++ b/solution.py
@@ -134,7 +134,7 @@
         jnp.einsum("mks,ks->m", weighted, extras[1], precision=lax.Precision.HIGHEST) * normalizer
     )
     gram_part, proj_part = (gram_part, proj_part)
-    gram_block, projection = lax.psum((gram_part, proj_part), ("lat", "lon"))
+    gram_block, projection = lax.psum(lax.psum((gram_part, proj_part), "lat"), "lon")
     return (fields[:members], fields[members], gram_block, projection, misfit_rows)
 
 

time: 560 us -> 352 us (0.63)
  the two profiles are of different devices: /device:TPU:258 before, /device:TPU:2 now
where the time goes in v1:
time: 352 us; the launch traced here: 351 us
  starting transfers between devices  162 us (46%)
  blocking collectives  107 us (30%)
  waiting for transfers between devices  25.8 us (7%)
  local copies, waits for them, and re-layouts  25.4 us (7%)
  matrix products  15.2 us (4%)
  other arithmetic  13.8 us (4%)
    psum x1, blocking collectives, on_device(): lax.psum(lax.psum((gram_part, proj_part), 'lat'), 'lon')  79.6 us
    ppermute x10, starting transfers between devices, padded_2(): lax.ppermute(tail, axis, [(i, (i + 1) % count) for i in range(ends)])  51.2 us
    ppermute x10, starting transfers between devices, padded_2(): lax.ppermute(head, axis, [((i + 1) % count, i) for i in range(ends)])  50.9 us
    all_to_all x1, starting transfers between devices, on_device(): lax.all_to_all(owner_misfit, ('lat', 'lon'), split_axis=0, concat_axis=0,...  24.7 us
    all_to_all x1, starting transfers between devices, on_device(): lax.all_to_all(send_records, ('lat', 'lon'), split_axis=0, concat_axis=0,...  21.5 us
    ppermute x10, waiting for transfers between devices, padded_2(): lax.ppermute(head, axis, [((i + 1) % count, i) for i in range(ends)])  17.8 us
    all_gather x1, blocking collectives, on_device(): green_all = lax.all_gather(green_cols, 'mem', axis=0, tiled=True)  14.4 us
    all_to_all x1, starting transfers between devices, on_device(): lax.all_to_all(send_ids, ('lat', 'lon'), split_axis=0, concat_axis=0, til...  13.9 us
  transfers between devices with their start and end apart: 23, of which 10 were waited for; matrix products, arithmetic and copies ran while one was open for 12% of the time, Pallas kernels for 0%

profile of v1, /device:TPU:2, one launch (start us, length us, event | category | flops | bytes accessed | tf_op | source)
XLA Modules:
  0.0 350.7 jit_solution(8631989751260173944)
XLA Ops:
  1.6 14.0 %collective-permute-start.1 = (bf16[3,100,1,128]{3,1,2,0:T(8,128)(2,1)S(1)}, bf16[3,100,1,128]{3,1,2,0:T(8,128)(2,1)S(1)}, u32[]{:S(2)}, u32[]{:S(2)}) collective-permute-start(bf16[3,100,1,128]{3,1,2,0:T(8,128)(2,1)S(1)} %broadcast_in_dim.30), channel_id=1, source_target_pairs={{1,0},{2,1},{3,2},{4,3},{5,4},{6,5},{7,6},{8,7},{9,8},{10,9},{11,1... | collective-permute-start | bytes 230408 | tf_op jit(solution)/shard_map/ppermute | solution.py:19
  15.6 1.9 collective-permute-start
  20.2 5.7 %collective-permute-done = bf16[3,100,1,128]{3,1,2,0:T(8,128)(2,1)S(1)} collective-permute-done((bf16[3,100,1,128]{3,1,2,0:T(8,128)(2,1)S(1)}, bf16[3,100,1,128]{3,1,2,0:T(8,128)(2,1)S(1)}, u32[]{:S(2)}, u32[]{:S(2)}) %collective-permute-start) | collective-permute-done | bytes 76832 | tf_op jit(solution)/shard_map/ppermute | solution.py:17
  28.9 5.6 %collective-permute-done.3 = bf16[3,100,6,1]{3,1,2,0:T(8,128)(2,1)S(1)} collective-permute-done((bf16[3,100,6,1]{3,1,2,0:T(8,128)(2,1)S(1)}, bf16[3,100,6,1]{3,1,2,0:T(8,128)(2,1)S(1)}, u32[]{:S(2)}, u32[]{:S(2)}) %collective-permute-start.3) | collective-permute-done | bytes 3632 | tf_op jit(solution)/shard_map/ppermute | solution.py:19
  35.2 1.6 fusion.19
  36.8 1.9 collective-permute-start.4
  38.7 7.8 %collective-permute-start.5 = (bf16[3,100,1,128]{3,1,2,0:T(8,128)(2,1)S(1)}, bf16[3,100,1,128]{3,1,2,0:T(8,128)(2,1)S(1)}, u32[]{:S(2)}, u32[]{:S(2)}) collective-permute-start(bf16[3,100,1,128]{3,1,2,0:T(8,128)(2,1)S(1)} %get-tuple-element.43), channel_id=1, source_target_pairs={{1,0},{2,1},{3,2},{4,3},{5,4},{6,5},{7,6},{8,7},{9,8},{10,9},{11,1... | collective-permute-start | bytes 230408 | tf_op jit(solution)/shard_map/ppermute | solution.py:19
  48.9 12.1 %collective-permute-start.6 = (bf16[3,100,6,1]{3,1,2,0:T(8,128)(2,1)S(1)}, bf16[3,100,6,1]{3,1,2,0:T(8,128)(2,1)S(1)}, u32[]{:S(2)}, u32[]{:S(2)}) collective-permute-start(bf16[3,100,6,1]{3,1,2,0:T(8,128)(2,1)S(1)} %get-tuple-element.32), channel_id=1, source_target_pairs={{0,32},{32,64},{64,96},{1,33},{33,65},{65,97},{2,34},{34,66},{66,9... | collective-permute-start | bytes 10808 | tf_op jit(solution)/shard_map/ppermute | solution.py:17
  64.6 13.9 %all-to-all-start.1 = ((s32[128,1,4]{2,1,0:T(1,128)}), s32[128,1,4]{2,1,0:T(1,128)S(1)}, u32[]{:S(2)}, u32[]{:S(2)}) async-start(s32[128,1,4]{2,1,0:T(1,128)} %bitcast.22), calls=%async_computation.1 | async-start | bytes 131072 | tf_op jit(solution)/shard_map/all_to_all | solution.py:97
  80.7 3.0 collective-permute-start.8
  83.8 6.7 %collective-permute-start.9 = (bf16[3,100,1,128]{3,1,2,0:T(8,128)(2,1)S(1)}, bf16[3,100,1,128]{3,1,2,0:T(8,128)(2,1)S(1)}, u32[]{:S(2)}, u32[]{:S(2)}) collective-permute-start(bf16[3,100,1,128]{3,1,2,0:T(8,128)(2,1)S(1)} %get-tuple-element.41), channel_id=1, source_target_pairs={{1,0},{2,1},{3,2},{4,3},{5,4},{6,5},{7,6},{8,7},{9,8},{10,9},{11,1... | collective-permute-start | bytes 230408 | tf_op jit(solution)/shard_map/ppermute | solution.py:19
  97.0 7.1 %scatter_fusion = f32[512,3,100]{2,1,0:T(4,128)S(1)} fusion(f32[512,3,100]{2,1,0:T(4,128)S(1)} %broadcast_in_dim.33, s32[256]{0:T(256)S(1)} %bitcast.104, f32[256,3,100]{2,1,0:T(4,128)S(1)} %copy.45), kind=kCustom, calls=%fused_computation.2 | custom fusion | bytes 922624 | tf_op jit(solution)/shard_map/scatter | solution.py:93
  107.3 1.9 collective-permute-start.12
  109.2 8.2 %collective-permute-start.13 = (bf16[3,100,1,128]{3,1,2,0:T(8,128)(2,1)S(1)}, bf16[3,100,1,128]{3,1,2,0:T(8,128)(2,1)S(1)}, u32[]{:S(2)}, u32[]{:S(2)}) collective-permute-start(bf16[3,100,1,128]{3,1,2,0:T(8,128)(2,1)S(1)} %get-tuple-element.39), channel_id=1, source_target_pairs={{1,0},{2,1},{3,2},{4,3},{5,4},{6,5},{7,6},{8,7},{9,8},{10,9},{11,1... | collective-permute-start | bytes 230408 | tf_op jit(solution)/shard_map/ppermute | solution.py:19
  117.5 21.5 %all-to-all-start = ((f32[128,4,3,100]{3,1,2,0:T(4,128)}), f32[128,4,3,100]{3,1,2,0:T(4,128)S(1)}, u32[]{:S(2)}, u32[]{:S(2)}) async-start(f32[128,4,3,100]{3,1,2,0:T(4,128)} %copy.47), calls=%async_computation | async-start | bytes 1572864 | tf_op jit(solution)/shard_map/all_to_all | solution.py:98
  139.5 1.7 collective-permute-start.14
  143.5 6.7 %collective-permute-done.15 = bf16[3,100,6,1]{3,1,2,0:T(8,128)(2,1)} collective-permute-done((bf16[3,100,6,1]{3,1,2,0:T(8,128)(2,1)S(1)}, bf16[3,100,6,1]{3,1,2,0:T(8,128)(2,1)}, u32[]{:S(2)}, u32[]{:S(2)}) %collective-permute-start.15) | collective-permute-done | bytes 3632 | tf_op jit(solution)/shard_map/ppermute | solution.py:19
  150.3 1.7 maximum_convert_fusion.3
  153.6 2.5 collective-permute-start.16
  156.1 7.3 %collective-permute-start.17 = (bf16[3,100,1,128]{3,1,2,0:T(8,128)(2,1)S(1)}, bf16[3,100,1,128]{3,1,2,0:T(8,128)(2,1)S(1)}, u32[]{:S(2)}, u32[]{:S(2)}) collective-permute-start(bf16[3,100,1,128]{3,1,2,0:T(8,128)(2,1)S(1)} %get-tuple-element.37), channel_id=1, source_target_pairs={{1,0},{2,1},{3,2},{4,3},{5,4},{6,5},{7,6},{8,7},{9,8},{10,9},{11,1... | collective-permute-start | bytes 230408 | tf_op jit(solution)/shard_map/ppermute | solution.py:19
  166.0 23.5 %collective-permute-start.18 = (bf16[3,100,6,1]{3,1,2,0:T(8,128)(2,1)S(1)}, bf16[3,100,6,1]{3,1,2,0:T(8,128)(2,1)S(1)}, u32[]{:S(2)}, u32[]{:S(2)}) collective-permute-start(bf16[3,100,6,1]{3,1,2,0:T(8,128)(2,1)S(1)} %get-tuple-element.26), channel_id=1, source_target_pairs={{0,32},{32,64},{64,96},{1,33},{33,65},{65,97},{2,34},{34,66},{66,9... | collective-permute-start | bytes 10808 | tf_op jit(solution)/shard_map/ppermute | solution.py:17
  192.1 1.7 collective-permute-done.19
  193.8 1.7 maximum_convert_fusion.4
  197.8 2.1 gather_fusion
  199.9 1.8 convert_bitcast_fusion
  204.7 1.9 fusion.36
  209.6 24.7 %all-to-all-start.2 = ((f32[128,4,100]{2,1,0:T(4,128)}), f32[128,4,100]{2,1,0:T(4,128)S(1)}, u32[]{:S(2)}, u32[]{:S(2)}) async-start(f32[128,4,100]{2,1,0:T(4,128)} %bitcast.35), calls=%async_computation.2 | async-start | bytes 524288 | tf_op jit(solution)/shard_map/all_to_all | solution.py:121
  235.5 14.4 %all_gather.3 = bf16[8,100,512]{2,1,0:T(8,128)(2,1)S(1)} all-gather(bf16[2,100,512]{2,1,0:T(8,128)(2,1)S(1)} %copy.52), channel_id=1, replica_groups=mesh['mem'=4,'lat'=4,'lon'=32] {'mem'}, dimensions={0}, use_global_device_ids=true | all-gather | bytes 1024000 | tf_op jit(solution)/shard_map/all_gather | solution.py:126
  250.1 3.9 %fusion.33 = f32[8]{0:T(128)S(1)} fusion(f32[100,512,1]{1,2,0:T(1,128)S(1)} %copy.60, f32[8,100,512]{2,1,0:T(8,128)S(1)} %convert_multiply_fusion), kind=kOutput, calls=%fused_computation.37 | convolution fusion | flops 4915208 | bytes 1843232 | tf_op jit(solution)/shard_map/mks,ks->m/dot_general | solution.py:134
  254.0 2.6 fusion.27
  256.5 13.0 %all-reduce.1 = (f32[8,8]{1,0:T(8,128)S(1)}, f32[8]{0:T(128)S(1)}) all-reduce(f32[8,8]{1,0:T(8,128)S(1)} %fusion.27, f32[8]{0:T(128)S(1)} %fusion.33), channel_id=1, replica_groups=mesh['mem'=4,'lat'=4,'lon'=32] {'lat'}, use_global_device_ids=true, to_apply=%region_5.6 | all-reduce | flops 72 | bytes 576 | tf_op jit(solution)/shard_map/psum | solution.py:137
  269.5 79.6 %all-reduce = (f32[8,8]{1,0:T(8,128)}, f32[8]{0:T(128)}) all-reduce(f32[8,8]{1,0:T(8,128)S(1)} %get-tuple-element.22, f32[8]{0:T(128)S(1)} %get-tuple-element.23), channel_id=1, replica_groups=mesh['mem'=4,'lat'=4,'lon'=32] {'lon'}, use_global_device_ids=true, to_apply=%region_6.7 | all-reduce | flops 72 | bytes 576 | tf_op jit(solution)/shard_map/psum | solution.py:137
  (127 shorter events, 45.6 us)
Async XLA Ops:
  0.6 18.0 %copy-start = (f32[16,100]{1,0:T(8,128)S(1)}, f32[16,100]{1,0:T(8,128)}, u32[]{:S(2)}) copy-start(f32[16,100]{1,0:T(8,128)} %param.14) | copy-start | bytes 19204
  1.6 18.6 %collective-permute-start.1 = (bf16[3,100,1,128]{3,1,2,0:T(8,128)(2,1)S(1)}, bf16[3,100,1,128]{3,1,2,0:T(8,128)(2,1)S(1)}, u32[]{:S(2)}, u32[]{:S(2)}) collective-permute-start(bf16[3,100,1,128]{3,1,2,0:T(8,128)(2,1)S(1)} %broadcast_in_dim.30), channel_id=1, source_target_pairs={{1,0},{2,1},{3,2},{4,3},{5,4},{6,5},{7,6},{8,7},{9,8},{10,9},{11,1... | collective-permute-start | bytes 230408 | tf_op jit(solution)/shard_map/ppermute | solution.py:19
  15.6 10.2 %collective-permute-start = (bf16[3,100,1,128]{3,1,2,0:T(8,128)(2,1)S(1)}, bf16[3,100,1,128]{3,1,2,0:T(8,128)(2,1)S(1)}, u32[]{:S(2)}, u32[]{:S(2)}) collective-permute-start(bf16[3,100,1,128]{3,1,2,0:T(8,128)(2,1)S(1)} %broadcast_in_dim.28), channel_id=1, source_target_pairs={{0,1},{1,2},{2,3},{3,4},{4,5},{5,6},{6,7},{7,8},{8,9},{9,10},{10,1... | collective-permute-start | bytes 230408 | tf_op jit(solution)/shard_map/ppermute | solution.py:17
  18.4 10.5 %copy-start.10 = (s32[4,128]{1,0:T(4,128)S(1)}, s32[4,128]{1,0:T(4,128)}, u32[]{:S(2)}) copy-start(s32[4,128]{1,0:T(4,128)} %param.13) | copy-start | bytes 6148
  18.4 10.5 %copy-start.8 = (bf16[2,100,100]{2,0,1:T(2,128)(2,1)S(1)}, bf16[2,100,100]{2,0,1:T(2,128)(2,1)}, u32[]{:S(2)}) copy-start(bf16[2,100,100]{2,0,1:T(2,128)(2,1)} %param.17) | copy-start | bytes 120004
  26.2 9.0 %copy-start.11 = (bf16[100,100]{1,0:T(8,128)(2,1)S(1)}, bf16[100,100]{1,0:T(8,128)(2,1)}, u32[]{:S(2)}) copy-start(bf16[100,100]{1,0:T(8,128)(2,1)} %param.18) | copy-start | bytes 60004
  26.2 2.8 collective-permute-start.2
  27.5 7.1 %collective-permute-start.3 = (bf16[3,100,6,1]{3,1,2,0:T(8,128)(2,1)S(1)}, bf16[3,100,6,1]{3,1,2,0:T(8,128)(2,1)S(1)}, u32[]{:S(2)}, u32[]{:S(2)}) collective-permute-start(bf16[3,100,6,1]{3,1,2,0:T(8,128)(2,1)S(1)} %get-tuple-element.35), channel_id=1, source_target_pairs={{32,0},{64,32},{96,64},{33,1},{65,33},{97,65},{34,2},{66,34},{98,6... | collective-permute-start | bytes 10808 | tf_op jit(solution)/shard_map/ppermute | solution.py:19
  35.2 11.4 %copy-start.9 = (s32[256,1]{0,1:T(1,128)S(1)}, s32[256,1]{0,1:T(1,128)}, u32[]{:S(2)}) copy-start(s32[256,1]{0,1:T(1,128)} %param.19) | copy-start | bytes 3076
  36.8 10.2 %collective-permute-start.4 = (bf16[3,100,1,128]{3,1,2,0:T(8,128)(2,1)S(1)}, bf16[3,100,1,128]{3,1,2,0:T(8,128)(2,1)S(1)}, u32[]{:S(2)}, u32[]{:S(2)}) collective-permute-start(bf16[3,100,1,128]{3,1,2,0:T(8,128)(2,1)S(1)} %get-tuple-element.42), channel_id=1, source_target_pairs={{0,1},{1,2},{2,3},{3,4},{4,5},{5,6},{6,7},{7,8},{8,9},{9,10},{10,1... | collective-permute-start | bytes 230408 | tf_op jit(solution)/shard_map/ppermute | solution.py:17
  38.7 9.9 %collective-permute-start.5 = (bf16[3,100,1,128]{3,1,2,0:T(8,128)(2,1)S(1)}, bf16[3,100,1,128]{3,1,2,0:T(8,128)(2,1)S(1)}, u32[]{:S(2)}, u32[]{:S(2)}) collective-permute-start(bf16[3,100,1,128]{3,1,2,0:T(8,128)(2,1)S(1)} %get-tuple-element.43), channel_id=1, source_target_pairs={{1,0},{2,1},{3,2},{4,3},{5,4},{6,5},{7,6},{8,7},{9,8},{10,9},{11,1... | collective-permute-start | bytes 230408 | tf_op jit(solution)/shard_map/ppermute | solution.py:19
  48.9 29.6 %collective-permute-start.6 = (bf16[3,100,6,1]{3,1,2,0:T(8,128)(2,1)S(1)}, bf16[3,100,6,1]{3,1,2,0:T(8,128)(2,1)S(1)}, u32[]{:S(2)}, u32[]{:S(2)}) collective-permute-start(bf16[3,100,6,1]{3,1,2,0:T(8,128)(2,1)S(1)} %get-tuple-element.32), channel_id=1, source_target_pairs={{0,32},{32,64},{64,96},{1,33},{33,65},{65,97},{2,34},{34,66},{66,9... | collective-permute-start | bytes 10808 | tf_op jit(solution)/shard_map/ppermute | solution.py:17
  61.0 17.5 %collective-permute-start.7 = (bf16[3,100,6,1]{3,1,2,0:T(8,128)(2,1)S(1)}, bf16[3,100,6,1]{3,1,2,0:T(8,128)(2,1)S(1)}, u32[]{:S(2)}, u32[]{:S(2)}) collective-permute-start(bf16[3,100,6,1]{3,1,2,0:T(8,128)(2,1)S(1)} %get-tuple-element.33), channel_id=1, source_target_pairs={{32,0},{64,32},{96,64},{33,1},{65,33},{97,65},{34,2},{66,34},{98,6... | collective-permute-start | bytes 10808 | tf_op jit(solution)/shard_map/ppermute | solution.py:19
  64.6 52.8 %all-to-all-start.1 = ((s32[128,1,4]{2,1,0:T(1,128)}), s32[128,1,4]{2,1,0:T(1,128)S(1)}, u32[]{:S(2)}, u32[]{:S(2)}) async-start(s32[128,1,4]{2,1,0:T(1,128)} %bitcast.22), calls=%async_computation.1 | async-start | bytes 131072 | tf_op jit(solution)/shard_map/all_to_all | solution.py:97
  79.1 11.4 %copy-start.5 = (f32[256,100]{0,1:T(8,128)S(1)}, f32[256,100]{0,1:T(8,128)}, u32[]{:S(2)}) copy-start(f32[256,100]{0,1:T(8,128)} %param.23) | copy-start | bytes 307204
  79.1 11.4 %copy-start.6 = (f32[256,100]{0,1:T(8,128)S(1)}, f32[256,100]{0,1:T(8,128)}, u32[]{:S(2)}) copy-start(f32[256,100]{0,1:T(8,128)} %param.22) | copy-start | bytes 307204
  79.1 11.4 %copy-start.7 = (f32[256,100]{0,1:T(8,128)S(1)}, f32[256,100]{0,1:T(8,128)}, u32[]{:S(2)}) copy-start(f32[256,100]{0,1:T(8,128)} %param.21) | copy-start | bytes 307204
  80.7 10.3 %collective-permute-start.8 = (bf16[3,100,1,128]{3,1,2,0:T(8,128)(2,1)S(1)}, bf16[3,100,1,128]{3,1,2,0:T(8,128)(2,1)S(1)}, u32[]{:S(2)}, u32[]{:S(2)}) collective-permute-start(bf16[3,100,1,128]{3,1,2,0:T(8,128)(2,1)S(1)} %get-tuple-element.40), channel_id=1, source_target_pairs={{0,1},{1,2},{2,3},{3,4},{4,5},{5,6},{6,7},{7,8},{8,9},{9,10},{10,1... | collective-permute-start | bytes 230408 | tf_op jit(solution)/shard_map/ppermute | solution.py:17
  83.8 8.7 %collective-permute-start.9 = (bf16[3,100,1,128]{3,1,2,0:T(8,128)(2,1)S(1)}, bf16[3,100,1,128]{3,1,2,0:T(8,128)(2,1)S(1)}, u32[]{:S(2)}, u32[]{:S(2)}) collective-permute-start(bf16[3,100,1,128]{3,1,2,0:T(8,128)(2,1)S(1)} %get-tuple-element.41), channel_id=1, source_target_pairs={{1,0},{2,1},{3,2},{4,3},{5,4},{6,5},{7,6},{8,7},{9,8},{10,9},{11,1... | collective-permute-start | bytes 230408 | tf_op jit(solution)/shard_map/ppermute | solution.py:19
  93.7 11.4 %collective-permute-start.10 = (bf16[3,100,6,1]{3,1,2,0:T(8,128)(2,1)}, bf16[3,100,6,1]{3,1,2,0:T(8,128)(2,1)S(1)}, u32[]{:S(2)}, u32[]{:S(2)}) collective-permute-start(bf16[3,100,6,1]{3,1,2,0:T(8,128)(2,1)} %get-tuple-element.30), channel_id=1, source_target_pairs={{0,32},{32,64},{64,96},{1,33},{33,65},{65,97},{2,34},{34,66},{66,9... | collective-permute-start | bytes 10808 | tf_op jit(solution)/shard_map/ppermute | solution.py:17
  95.1 10.1 %collective-permute-start.11 = (bf16[3,100,6,1]{3,1,2,0:T(8,128)(2,1)}, bf16[3,100,6,1]{3,1,2,0:T(8,128)(2,1)S(1)}, u32[]{:S(2)}, u32[]{:S(2)}) collective-permute-start(bf16[3,100,6,1]{3,1,2,0:T(8,128)(2,1)} %get-tuple-element.31), channel_id=1, source_target_pairs={{32,0},{64,32},{96,64},{33,1},{65,33},{97,65},{34,2},{66,34},{98,6... | collective-permute-start | bytes 10808 | tf_op jit(solution)/shard_map/ppermute | solution.py:19
  107.3 31.9 %collective-permute-start.12 = (bf16[3,100,1,128]{3,1,2,0:T(8,128)(2,1)S(1)}, bf16[3,100,1,128]{3,1,2,0:T(8,128)(2,1)S(1)}, u32[]{:S(2)}, u32[]{:S(2)}) collective-permute-start(bf16[3,100,1,128]{3,1,2,0:T(8,128)(2,1)S(1)} %get-tuple-element.38), channel_id=1, source_target_pairs={{0,1},{1,2},{2,3},{3,4},{4,5},{5,6},{6,7},{7,8},{8,9},{9,10},{10,1... | collective-permute-start | bytes 230408 | tf_op jit(solution)/shard_map/ppermute | solution.py:17
  109.2 30.0 %collective-permute-start.13 = (bf16[3,100,1,128]{3,1,2,0:T(8,128)(2,1)S(1)}, bf16[3,100,1,128]{3,1,2,0:T(8,128)(2,1)S(1)}, u32[]{:S(2)}, u32[]{:S(2)}) collective-permute-start(bf16[3,100,1,128]{3,1,2,0:T(8,128)(2,1)S(1)} %get-tuple-element.39), channel_id=1, source_target_pairs={{1,0},{2,1},{3,2},{4,3},{5,4},{6,5},{7,6},{8,7},{9,8},{10,9},{11,1... | collective-permute-start | bytes 230408 | tf_op jit(solution)/shard_map/ppermute | solution.py:19
  117.5 86.9 %all-to-all-start = ((f32[128,4,3,100]{3,1,2,0:T(4,128)}), f32[128,4,3,100]{3,1,2,0:T(4,128)S(1)}, u32[]{:S(2)}, u32[]{:S(2)}) async-start(f32[128,4,3,100]{3,1,2,0:T(4,128)} %copy.47), calls=%async_computation | async-start | bytes 1572864 | tf_op jit(solution)/shard_map/all_to_all | solution.py:98
  139.5 3.3 collective-permute-start.14
  141.1 9.1 %collective-permute-start.15 = (bf16[3,100,6,1]{3,1,2,0:T(8,128)(2,1)S(1)}, bf16[3,100,6,1]{3,1,2,0:T(8,128)(2,1)}, u32[]{:S(2)}, u32[]{:S(2)}) collective-permute-start(bf16[3,100,6,1]{3,1,2,0:T(8,128)(2,1)S(1)} %get-tuple-element.29), channel_id=1, source_target_pairs={{32,0},{64,32},{96,64},{33,1},{65,33},{97,65},{34,2},{66,34},{98,6... | collective-permute-start | bytes 10808 | tf_op jit(solution)/shard_map/ppermute | solution.py:19
  153.6 11.6 %collective-permute-start.16 = (bf16[3,100,1,128]{3,1,2,0:T(8,128)(2,1)S(1)}, bf16[3,100,1,128]{3,1,2,0:T(8,128)(2,1)S(1)}, u32[]{:S(2)}, u32[]{:S(2)}) collective-permute-start(bf16[3,100,1,128]{3,1,2,0:T(8,128)(2,1)S(1)} %get-tuple-element.36), channel_id=1, source_target_pairs={{0,1},{1,2},{2,3},{3,4},{4,5},{5,6},{6,7},{7,8},{8,9},{9,10},{10,1... | collective-permute-start | bytes 230408 | tf_op jit(solution)/shard_map/ppermute | solution.py:17
  156.1 9.7 %collective-permute-start.17 = (bf16[3,100,1,128]{3,1,2,0:T(8,128)(2,1)S(1)}, bf16[3,100,1,128]{3,1,2,0:T(8,128)(2,1)S(1)}, u32[]{:S(2)}, u32[]{:S(2)}) collective-permute-start(bf16[3,100,1,128]{3,1,2,0:T(8,128)(2,1)S(1)} %get-tuple-element.37), channel_id=1, source_target_pairs={{1,0},{2,1},{3,2},{4,3},{5,4},{6,5},{7,6},{8,7},{9,8},{10,9},{11,1... | collective-permute-start | bytes 230408 | tf_op jit(solution)/shard_map/ppermute | solution.py:19
  166.0 25.3 %collective-permute-start.18 = (bf16[3,100,6,1]{3,1,2,0:T(8,128)(2,1)S(1)}, bf16[3,100,6,1]{3,1,2,0:T(8,128)(2,1)S(1)}, u32[]{:S(2)}, u32[]{:S(2)}) collective-permute-start(bf16[3,100,6,1]{3,1,2,0:T(8,128)(2,1)S(1)} %get-tuple-element.26), channel_id=1, source_target_pairs={{0,32},{32,64},{64,96},{1,33},{33,65},{65,97},{2,34},{34,66},{66,9... | collective-permute-start | bytes 10808 | tf_op jit(solution)/shard_map/ppermute | solution.py:17
  189.5 4.2 %collective-permute-start.19 = (bf16[3,100,6,1]{3,1,2,0:T(8,128)(2,1)S(1)}, bf16[3,100,6,1]{3,1,2,0:T(8,128)(2,1)}, u32[]{:S(2)}, u32[]{:S(2)}) collective-permute-start(bf16[3,100,6,1]{3,1,2,0:T(8,128)(2,1)S(1)} %get-tuple-element.27), channel_id=1, source_target_pairs={{32,0},{64,32},{96,64},{33,1},{65,33},{97,65},{34,2},{66,34},{98,6... | collective-permute-start | bytes 10808 | tf_op jit(solution)/shard_map/ppermute | solution.py:19
  201.7 1.9 slice-start
  209.6 139.5 %all-to-all-start.2 = ((f32[128,4,100]{2,1,0:T(4,128)}), f32[128,4,100]{2,1,0:T(4,128)S(1)}, u32[]{:S(2)}, u32[]{:S(2)}) async-start(f32[128,4,100]{2,1,0:T(4,128)} %bitcast.35), calls=%async_computation.2 | async-start | bytes 524288 | tf_op jit(solution)/shard_map/all_to_all | solution.py:121
  (4 other events, 3.5 us)
